TPU v7x, 32 devices: a whole 2x2x4 slice. The times are simulated.
32 devices in a mesh: freq: 4 (over x, core), tm: 8 (over z, y).
Axes of the slice: x: 2, y: 2, z: 4, core: 2. Of those that a mesh axis runs over, the one named last changes fastest.
Arguments:
- visibilities: float32 [8, 8, 1024], P('freq', None, 'tm'), may hold values from -6 to 6
- coherencies: bfloat16 [8, 8, 8, 1024], P('freq', None, None, 'tm'), may hold values from -2.09375 to 2.09375
- pairs: int32 [2, 1024], P(None, 'tm'), may hold values from 0 to 511, as said below
- gains_start: float32 [8, 8, 8, 512], P('freq'), may hold values from -0.9 to 1.9
- duals_start: float32 [8, 8, 8, 512], P('freq'), may hold values from -12 to 12
- poly_start: float32 [4, 8, 8, 512], replicated, may hold values from -0.6 to 1.6
Outputs:
- gains: float32 [8, 8, 8, 512], P('freq')
- duals: float32 [8, 8, 8, 512], P('freq')
- polynomial: float32 [4, 8, 8, 512], replicated
Inputs may be any that keep to these rules, and one draw needn't show every extreme that they name: `pairs`: each row names two different stations.
All inputs are finite; a program needn't handle non-finite values.
Results may differ from a plain program's by a relative error of at most 0.0003.
Values sent between devices are 32-bit elements; how exact they have to be, the bound alone decides.
A program may use at most 64 MiB of HBM per device.

v0:
```python
from functools import partial
import jax
import jax.numpy as jnp
from jax import lax
from jax.sharding import PartitionSpec as P

ITERS = 2
RHO = 16.0
HIGHEST = lax.Precision.HIGHEST


def split(block):
    return ([block[i] for i in range(4)], [block[i + 4] for i in range(4)])


def join(matrix):
    return jnp.stack(matrix[0] + matrix[1])


def adjoint(matrix):
    real_part, imag_part = matrix
    return (
        [real_part[0], real_part[2], real_part[1], real_part[3]],
        [-imag_part[0], -imag_part[2], -imag_part[1], -imag_part[3]],
    )


def product(left, right):
    left_real, left_imag = left
    right_real, right_imag = right
    out_real = []
    out_imag = []
    for row in range(2):
        for column in range(2):
            first = 2 * row
            out_real.append(
                left_real[first] * right_real[column]
                - left_imag[first] * right_imag[column]
                + left_real[first + 1] * right_real[column + 2]
                - left_imag[first + 1] * right_imag[column + 2]
            )
            out_imag.append(
                left_real[first] * right_imag[column]
                + left_imag[first] * right_real[column]
                + left_real[first + 1] * right_imag[column + 2]
                + left_imag[first + 1] * right_real[column + 2]
            )
    return (out_real, out_imag)


def normal(matrix):
    real_part, imag_part = matrix
    top_left = real_part[0] ** 2 + imag_part[0] ** 2 + real_part[1] ** 2 + imag_part[1] ** 2
    bottom_right = real_part[2] ** 2 + imag_part[2] ** 2 + real_part[3] ** 2 + imag_part[3] ** 2
    cross_real = (
        real_part[0] * real_part[2]
        + imag_part[0] * imag_part[2]
        + real_part[1] * real_part[3]
        + imag_part[1] * imag_part[3]
    )
    cross_imag = (
        imag_part[0] * real_part[2]
        - real_part[0] * imag_part[2]
        + imag_part[1] * real_part[3]
        - real_part[1] * imag_part[3]
    )
    return jnp.stack([top_left, bottom_right, cross_real, cross_imag])


def data_sums(gains, coherencies, visibilities, pairs):
    jones_first = split(jnp.take(gains, pairs[0], axis=2))
    jones_second = split(jnp.take(gains, pairs[1], axis=2))
    skymodel = split(coherencies.astype(jnp.float32))
    left = product(jones_first, skymodel)
    right = product(skymodel, adjoint(jones_second))
    model = jnp.sum(join(product(left, adjoint(jones_second))), axis=1)
    residual = split((visibilities - model)[:, None, :])
    first_terms = jnp.concatenate([join(product(residual, adjoint(right))), normal(right)], axis=0)
    second_terms = jnp.concatenate(
        [join(product(adjoint(residual), left)), normal(adjoint(left))], axis=0
    )
    terms = jnp.concatenate([first_terms, second_terms], axis=2)
    stations = jnp.concatenate([pairs[0], pairs[1]])
    flat = terms.reshape(-1, terms.shape[2]).T
    summed = jax.ops.segment_sum(flat, stations, num_segments=gains.shape[2])
    return summed.T.reshape(12, gains.shape[1], gains.shape[2])


def update(gains, duals, prior, sums, damping):
    direction = split(sums[:8] - duals - RHO * (gains - prior))
    top_left, bottom_right, cross_real, cross_imag = (sums[8], sums[9], sums[10], sums[11])
    shift = damping * 0.5 * (top_left + bottom_right) + RHO
    upper = top_left + shift
    lower = bottom_right + shift
    determinant = upper * lower - cross_real * cross_real - cross_imag * cross_imag
    zeros = jnp.zeros_like(determinant)
    inverse = (
        [
            lower / determinant,
            -cross_real / determinant,
            -cross_real / determinant,
            upper / determinant,
        ],
        [zeros, -cross_imag / determinant, cross_imag / determinant, zeros],
    )
    return gains + join(product(direction, inverse))


def basis_weights(count):
    position = (2.0 * jnp.arange(count).astype(jnp.float32) + 1.0) / count - 1.0
    basis = jnp.stack(
        [
            jnp.ones_like(position),
            position,
            1.5 * position * position - 0.5,
            2.5 * position * position * position - 1.5 * position,
        ],
        axis=1,
    )
    gram = jnp.dot(basis.T, basis, precision=HIGHEST)
    factor = jnp.linalg.cholesky(gram)
    weights = jax.scipy.linalg.cho_solve((factor, True), basis.T)
    return (basis, weights)


def shards(visibilities, coherencies, pairs, gains_start, duals_start, poly_start):
    channels = gains_start.shape[0]
    offset = lax.axis_index("freq") * channels
    basis, weights = basis_weights(channels * lax.axis_size("freq"))
    local_basis = lax.dynamic_slice_in_dim(basis, offset, channels, 0)
    local_weights = lax.dynamic_slice_in_dim(weights, offset, channels, 1)
    channel_sums = jax.vmap(data_sums, in_axes=(0, 0, 0, None))
    gains, duals = (gains_start, duals_start)
    prior = jnp.einsum("fj,jcks->fcks", local_basis, poly_start, precision=HIGHEST)
    for inner in range(ITERS):
        local_terms = channel_sums(gains, coherencies, visibilities, pairs)
        sums = lax.psum(local_terms, "tm")
        gains = jax.vmap(partial(update, damping=12.0 * 0.5**inner))(gains, duals, prior, sums)
    mixed = gains + duals / RHO
    partial_fit = jnp.einsum("jf,fcks->jcks", local_weights, mixed, precision=HIGHEST)
    polynomial = lax.psum(partial_fit, "freq")
    prior = jnp.einsum("fj,jcks->fcks", local_basis, polynomial, precision=HIGHEST)
    duals = duals + RHO * (gains - prior)
    return (gains, duals, polynomial)


def solution(mesh):
    placed = (
        P("freq", None, "tm"),
        P("freq", None, None, "tm"),
        P(None, "tm"),
        P("freq", None, None, None),
        P("freq", None, None, None),
        P(),
    )
    return jax.shard_map(
        shards,
        mesh=mesh,
        in_specs=placed,
        out_specs=(P("freq", None, None, None), P("freq", None, None, None), P()),
        check_vma=False,
    )
```

profile of v0, /device:TPU:0, one launch (start us, length us, event | category | flops | bytes accessed | tf_op | source)
XLA Modules:
  0.0 250.6 jit_solution(10916335076422849878)
XLA Ops:
  7.2 0.8 compare_and_fusion.1
  8.0 3.5 %copy.795 = f32[2,8,8,512]{2,1,3,0:T(8,128)} copy(f32[2,8,8,512]{3,2,1,0:T(8,128)} %param.11) | data formatting | bytes 524288 | tf_op args[3]
  11.5 2.9 %gather_fusion.1 = f32[128,2,8,8]{3,2,1,0:T(8,128)S(1)} fusion(f32[2,8,8,512]{2,1,3,0:T(8,128)} %copy.795, s32[1024]{0:T(1024)S(1)} %pad_clamp_fusion), kind=kCustom, calls=%fused_computation.1.clone | custom fusion | bytes 131584 | tf_op jit(solution)/shard_map/vmap(jit(_take))/gather | solution.py:72
  14.4 0.4 copy.799
  14.8 2.9 %gather_fusion = f32[128,2,8,8]{3,2,1,0:T(8,128)S(1)} fusion(f32[2,8,8,512]{2,1,3,0:T(8,128)} %copy.795, s32[1024]{0:T(1024)S(1)} %pad_clamp_fusion.1), kind=kCustom, calls=%fused_computation.clone | custom fusion | bytes 131584 | tf_op jit(solution)/shard_map/vmap(jit(_take))/gather | solution.py:71
  17.7 0.4 copy.796
  20.6 8.3 %scatter_fusion = f32[2,512,96]{2,0,1:T(2,128)S(1)} fusion(f32[2,512,96]{2,0,1:T(2,128)S(1)} %broadcast.1350.clone, s32[256]{0:T(256)S(1)} %pad_add_fusion, f32[256,2,96]{2,1,0:T(2,128)S(1)} %copy.818), kind=kCustom, calls=%fused_computation.4 | custom fusion | flops 49152 | bytes 590848 | tf_op jit(solution)/shard_map/vmap()/scatter-add | solution.py:85
  29.2 0.8 copy.820
  30.9 0.6 compare_reduce_fusion
  31.5 0.6 fusion.31
  32.5 1.2 fusion.2
  33.8 70.9 %all-reduce.4.cloned.1.call-done = f32[2,12,8,512]{3,2,0,1:T(8,128)} async-done(((f32[2,12,8,512]{3,2,0,1:T(8,128)}), f32[2,12,8,512]{3,2,0,1:T(8,128)}) %all-reduce.4.cloned.1.call-update) | async-done | bytes 393232 | tf_op jit(solution)/shard_map/psum | solution.py:137
  104.7 1.1 fusion.5
  105.8 0.8 constant_dynamic-update-slice_fusion.31
  106.6 0.8 constant_dynamic-update-slice_fusion.30
  107.7 2.6 %copy.826 = f32[2,8,8,512]{2,1,3,0:T(8,128)} copy(f32[2,8,8,512]{3,2,0,1:T(8,128)S(1)} %bitcast_add_fusion.1) | data formatting | bytes 524288 | tf_op jit(solution)/shard_map/vmap()/add | solution.py:106
  110.3 2.9 %gather_fusion.2 = f32[128,2,8,8]{3,2,1,0:T(8,128)S(1)} fusion(f32[2,8,8,512]{2,1,3,0:T(8,128)} %copy.826, s32[1024]{0:T(1024)S(1)} %pad_clamp_fusion.1), kind=kCustom, calls=%fused_computation.2.clone | custom fusion | bytes 131584 | tf_op jit(solution)/shard_map/vmap(jit(_take))/gather | solution.py:71
  113.2 3.8 %gather_fusion.3 = f32[128,2,8,8]{3,2,1,0:T(8,128)} fusion(f32[2,8,8,512]{2,1,3,0:T(8,128)} %copy.826, s32[1024]{0:T(1024)S(1)} %pad_clamp_fusion), kind=kCustom, calls=%fused_computation.3.clone | custom fusion | bytes 131584 | tf_op jit(solution)/shard_map/vmap(jit(_take))/gather | solution.py:72
  117.0 0.4 copy.827
  117.4 1.6 copy.829
  121.2 8.3 %scatter_fusion.1 = f32[2,512,96]{2,0,1:T(2,128)S(1)} fusion(f32[2,512,96]{2,0,1:T(2,128)S(1)} %broadcast.1350, s32[256]{0:T(256)S(1)} %pad_add_fusion, f32[256,2,96]{2,1,0:T(2,128)S(1)} %copy.848), kind=kCustom, calls=%fused_computation.5 | custom fusion | flops 49152 | bytes 590848 | tf_op jit(solution)/shard_map/vmap()/scatter-add | solution.py:85
  129.7 0.8 copy.850
  131.2 70.4 %all-reduce.6.cloned.1.call-done = f32[2,12,8,512]{3,2,0,1:T(8,128)} async-done(((f32[2,12,8,512]{3,2,0,1:T(8,128)}), f32[2,12,8,512]{3,2,0,1:T(8,128)}) %all-reduce.6.cloned.1.call-update) | async-done | bytes 393232 | tf_op jit(solution)/shard_map/psum | solution.py:137
  201.5 1.1 fusion.4
  202.6 0.8 constant_dynamic-update-slice_fusion.63
  203.4 0.8 constant_dynamic-update-slice_fusion.62
  204.5 2.1 fusion.8
  206.6 0.7 copy.859
  207.3 31.9 %all-reduce.8.cloned.1.call-done = f32[4,8,8,512]{3,0,2,1:T(4,128)} async-done(((f32[4,8,8,512]{3,0,2,1:T(4,128)}), f32[4,8,8,512]{3,0,2,1:T(4,128)}) %all-reduce.8.cloned.1.call-update) | async-done | bytes 524304 | tf_op jit(solution)/shard_map/psum | solution.py:141
  239.2 2.0 fusion.38
  241.4 0.7 copy.860
  242.1 2.0 copy.861
  (147 shorter events, 6.9 us)
Async XLA Ops:
  7.2 25.3 %copy-start = (f32[4,8,8,512]{3,2,1,0:T(8,128)S(1)}, f32[4,8,8,512]{3,2,1,0:T(8,128)}, u32[]{:S(2)}) copy-start(f32[4,8,8,512]{3,2,1,0:T(8,128)} %param.13) | copy-start | bytes 1572868
  7.2 10.9 %copy-start.3 = (bf16[2,8,8,128]{3,2,1,0:T(8,128)(2,1)S(1)}, bf16[2,8,8,128]{3,2,1,0:T(8,128)(2,1)}, u32[]{:S(2)}) copy-start(bf16[2,8,8,128]{3,2,1,0:T(8,128)(2,1)} %param.9) | copy-start | bytes 98308
  7.2 97.5 %all-reduce.4.cloned.1.call-start = ((), (), s32[]{:S(2)}) async-start(), calls=%async_computation | async-start | bytes 786432 | tf_op jit(solution)/shard_map/psum | solution.py:137
  8.0 10.6 %copy-start.4 = (f32[2,8,128]{2,1,0:T(8,128)S(1)}, f32[2,8,128]{2,1,0:T(8,128)}, u32[]{:S(2)}) copy-start(f32[2,8,128]{2,1,0:T(8,128)} %param.8) | copy-start | bytes 24580
  11.5 7.5 %copy-start.5 = (s32[2,128]{1,0:T(2,128)S(1)}, s32[2,128]{1,0:T(2,128)}, u32[]{:S(2)}) copy-start(s32[2,128]{1,0:T(2,128)} %param.10) | copy-start | bytes 3076
  18.9 85.8 %copy-start.1 = (f32[2,8,8,512]{3,2,1,0:T(8,128)S(1)}, f32[2,8,8,512]{3,2,1,0:T(8,128)}, u32[]{:S(2)}) copy-start(f32[2,8,8,512]{3,2,1,0:T(8,128)} %param.12) | copy-start | bytes 786436
  18.9 85.8 %copy-start.2 = (f32[2,8,8,512]{3,2,1,0:T(8,128)S(1)}, f32[2,8,8,512]{3,2,1,0:T(8,128)}, u32[]{:S(2)}) copy-start(f32[2,8,8,512]{3,2,1,0:T(8,128)} %param.11) | copy-start | bytes 786436
  30.0 171.6 %all-reduce.6.cloned.1.call-start = ((), (), s32[]{:S(2)}) async-start(), calls=%async_computation.1 | async-start | bytes 786432 | tf_op jit(solution)/shard_map/psum | solution.py:137
  130.5 108.7 %all-reduce.8.cloned.1.call-start = ((), (), s32[]{:S(2)}) async-start(), calls=%async_computation.2 | async-start | bytes 1048576 | tf_op jit(solution)/shard_map/psum | solution.py:141
Sparse Core Ops, SparseCore 0:
  30.1 74.5 all-reduce.3
  130.7 70.8 all-reduce.5
  206.7 32.4 all-reduce.7
where the time goes:
time: 251 us
  waiting for transfers between devices  173 us (69%)
  local copies, waits for them, and re-layouts  30 us (12%)
  other arithmetic  26.6 us (11%)
  between operations  14.6 us (6%)
  matrix products  5.93 us (2%)
    psum x2, waiting for transfers between devices, shards(): sums = lax.psum(local_terms, 'tm')  141 us
    psum x1, waiting for transfers between devices, shards(): polynomial = lax.psum(partial_fit, 'freq')  31.9 us
    scatter-add x2, other arithmetic, data_sums(): summed = jax.ops.segment_sum(flat, stations, num_segments=gains.shape[2])  16.7 us
    gather x4, local copies, waits for them, and re-layouts, data_sums(): jones_second = split(jnp.take(gains, pairs[1], axis=2))  8.74 us
    unnamed x19, local copies, waits for them, and re-layouts  7.63 us
    gather x4, local copies, waits for them, and re-layouts, data_sums(): jones_first = split(jnp.take(gains, pairs[0], axis=2))  6.57 us
  transfers between devices with their start and end apart: 3, of which 3 were waited for; matrix products, arithmetic and copies ran while one was open for 2% of the time, Pallas kernels for 0%

commit v1 on v0

--- a/solution.py
+++ b/solution.py
@@ -134,7 +134,11 @@
     prior = jnp.einsum("fj,jcks->fcks", local_basis, poly_start, precision=HIGHEST)
     for inner in range(ITERS):
         local_terms = channel_sums(gains, coherencies, visibilities, pairs)
-        sums = lax.psum(local_terms, "tm")
+
+        def guide_halves_over_axis(lane_axis, mine_x):
+            return jnp.sum(lax.all_gather(mine_x, axis_name=lane_axis), axis=0)
+
+        sums = guide_halves_over_axis("tm", local_terms)
         gains = jax.vmap(partial(update, damping=12.0 * 0.5**inner))(gains, duals, prior, sums)
     mixed = gains + duals / RHO
     partial_fit = jnp.einsum("jf,fcks->jcks", local_weights, mixed, precision=HIGHEST)

time: 251 us -> 226 us (0.900)
  waiting for transfers between devices: 173 us -> 149 us
    psum x2 -> x0, waiting for transfers between devices: 141 us -> none  [shards(): sums = lax.psum(local_terms, 'tm')]
    all_gather x0 -> x2, waiting for transfers between devices: none -> 117 us  [guide_halves_over_axis(): return jnp.sum(lax.all_gather(mine_x, axis_name=lane_axis), axis=0)]
    reduce_sum x0 -> x2, other arithmetic: none -> 4.53 us  [guide_halves_over_axis(): return jnp.sum(lax.all_gather(mine_x, axis_name=lane_axis), axis=0)]
    unnamed x54, other arithmetic: 4.19 us -> 0.99 us
where the time goes in v1:
time: 226 us
  waiting for transfers between devices  149 us (66%)
  local copies, waits for them, and re-layouts  29.9 us (13%)
  other arithmetic  26 us (12%)
  between operations  14.6 us (6%)
  matrix products  5.95 us (3%)
    all_gather x2, waiting for transfers between devices, guide_halves_over_axis(): return jnp.sum(lax.all_gather(mine_x, axis_name=lane_axis), axis=0)  117 us
    psum x1, waiting for transfers between devices, shards(): polynomial = lax.psum(partial_fit, 'freq')  31.5 us
    scatter-add x2, other arithmetic, data_sums(): summed = jax.ops.segment_sum(flat, stations, num_segments=gains.shape[2])  16.7 us
    gather x4, local copies, waits for them, and re-layouts, data_sums(): jones_second = split(jnp.take(gains, pairs[1], axis=2))  8.74 us
    unnamed x19, local copies, waits for them, and re-layouts  7.63 us
    gather x4, local copies, waits for them, and re-layouts, data_sums(): jones_first = split(jnp.take(gains, pairs[0], axis=2))  6.57 us
    reduce_sum x2, other arithmetic, guide_halves_over_axis(): return jnp.sum(lax.all_gather(mine_x, axis_name=lane_axis), axis=0)  4.53 us
  transfers between devices with their start and end apart: 3, of which 3 were waited for; matrix products, arithmetic and copies ran while one was open for 2% of the time, Pallas kernels for 0%

profile of v1, /device:TPU:0, one launch (start us, length us, event | category | flops | bytes accessed | tf_op | source)
XLA Modules:
  0.0 225.7 jit_solution(9591774348343620963)
XLA Ops:
  7.2 0.8 compare_and_fusion.1
  8.0 3.5 %copy.750 = f32[2,8,8,512]{2,1,3,0:T(8,128)} copy(f32[2,8,8,512]{3,2,1,0:T(8,128)} %param.11) | data formatting | bytes 524288 | tf_op args[3]
  11.5 2.9 %gather_fusion.1 = f32[128,2,8,8]{3,2,1,0:T(8,128)S(1)} fusion(f32[2,8,8,512]{2,1,3,0:T(8,128)} %copy.750, s32[1024]{0:T(1024)S(1)} %pad_clamp_fusion), kind=kCustom, calls=%fused_computation.1.clone | custom fusion | bytes 131584 | tf_op jit(solution)/shard_map/vmap(jit(_take))/gather | solution.py:72
  14.4 0.4 copy.754
  14.8 2.9 %gather_fusion = f32[128,2,8,8]{3,2,1,0:T(8,128)S(1)} fusion(f32[2,8,8,512]{2,1,3,0:T(8,128)} %copy.750, s32[1024]{0:T(1024)S(1)} %pad_clamp_fusion.1), kind=kCustom, calls=%fused_computation.clone | custom fusion | bytes 131584 | tf_op jit(solution)/shard_map/vmap(jit(_take))/gather | solution.py:71
  17.7 0.4 copy.751
  18.4 0.2 copy.833
  20.6 8.3 %scatter_fusion = f32[2,512,96]{2,0,1:T(2,128)S(1)} fusion(f32[2,512,96]{2,0,1:T(2,128)S(1)} %broadcast.1350.clone, s32[256]{0:T(256)S(1)} %pad_add_fusion, f32[256,2,96]{2,1,0:T(2,128)S(1)} %copy.773), kind=kCustom, calls=%fused_computation.4 | custom fusion | flops 49152 | bytes 590848 | tf_op jit(solution)/shard_map/vmap()/scatter-add | solution.py:85
  29.0 0.9 copy.774
  30.1 1.2 fusion.2
  31.4 61.5 %all-gather.3.cloned.1.call-done = f32[8,2,12,8,512]{4,3,2,1,0:T(8,128)} async-done(((f32[1,2,12,8,512]{4,3,2,1,0:T(8,128)}), f32[8,2,12,8,512]{4,3,2,1,0:T(8,128)}) %all-gather.3.cloned.1.call-update) | async-done | bytes 3145744 | tf_op jit(solution)/shard_map/all_gather | solution.py:139
  92.8 2.3 %reduce_sum.37 = f32[2,12,8,512]{3,2,1,0:T(8,128)S(1)} reduce(f32[8,2,12,8,512]{4,3,2,1,0:T(8,128)} %all-gather.3.cloned.1.call-done, f32[]{:T(128)} %constant.80.clone.1), dimensions={0}, to_apply=%region_2.4 | reduce | flops 688128 | bytes 3538948 | tf_op jit(solution)/shard_map/reduce_sum | solution.py:139
  95.6 2.6 %copy.785 = f32[2,8,8,512]{2,1,3,0:T(8,128)} copy(f32[2,8,8,512]{3,2,0,1:T(8,128)S(1)} %bitcast_add_fusion.1) | data formatting | bytes 524288 | tf_op jit(solution)/shard_map/vmap()/add | solution.py:106
  98.2 2.9 %gather_fusion.2 = f32[128,2,8,8]{3,2,1,0:T(8,128)S(1)} fusion(f32[2,8,8,512]{2,1,3,0:T(8,128)} %copy.785, s32[1024]{0:T(1024)S(1)} %pad_clamp_fusion.1), kind=kCustom, calls=%fused_computation.2.clone | custom fusion | bytes 131584 | tf_op jit(solution)/shard_map/vmap(jit(_take))/gather | solution.py:71
  101.0 3.8 %gather_fusion.3 = f32[128,2,8,8]{3,2,1,0:T(8,128)} fusion(f32[2,8,8,512]{2,1,3,0:T(8,128)} %copy.785, s32[1024]{0:T(1024)S(1)} %pad_clamp_fusion), kind=kCustom, calls=%fused_computation.3.clone | custom fusion | bytes 131584 | tf_op jit(solution)/shard_map/vmap(jit(_take))/gather | solution.py:72
  104.9 0.4 copy.786
  105.3 1.6 copy.788
  107.1 0.2 copy.834
  109.1 8.3 %scatter_fusion.1 = f32[2,512,96]{2,0,1:T(2,128)S(1)} fusion(f32[2,512,96]{2,0,1:T(2,128)S(1)} %broadcast.1350, s32[256]{0:T(256)S(1)} %pad_add_fusion, f32[256,2,96]{2,1,0:T(2,128)S(1)} %copy.807), kind=kCustom, calls=%fused_computation.5 | custom fusion | flops 49152 | bytes 590848 | tf_op jit(solution)/shard_map/vmap()/scatter-add | solution.py:85
  117.4 0.9 copy.808
  118.9 0.4 cholesky.16
  119.3 0.6 compare_reduce_fusion
  120.0 0.6 fusion.31
  120.6 0.3 custom-call.10
  121.4 55.9 %all-gather.5.cloned.1.call-done = f32[8,2,12,8,512]{4,3,2,1,0:T(8,128)} async-done(((f32[1,2,12,8,512]{4,3,2,1,0:T(8,128)}), f32[8,2,12,8,512]{4,3,2,1,0:T(8,128)}) %all-gather.5.cloned.1.call-update) | async-done | bytes 3145744 | tf_op jit(solution)/shard_map/all_gather | solution.py:139
  177.2 2.3 %reduce_sum.39 = f32[2,12,8,512]{3,2,1,0:T(8,128)S(1)} reduce(f32[8,2,12,8,512]{4,3,2,1,0:T(8,128)} %all-gather.5.cloned.1.call-done, f32[]{:T(128)} %constant.80.clone.1), dimensions={0}, to_apply=%region_5.7 | reduce | flops 688128 | bytes 3538948 | tf_op jit(solution)/shard_map/reduce_sum | solution.py:139
  179.9 2.1 fusion.8
  182.1 0.7 copy.822
  182.8 31.5 %all-reduce.2.cloned.1.call-done = f32[4,8,8,512]{3,0,2,1:T(4,128)} async-done(((f32[4,8,8,512]{3,0,2,1:T(4,128)}), f32[4,8,8,512]{3,0,2,1:T(4,128)}) %all-reduce.2.cloned.1.call-update) | async-done | bytes 524304 | tf_op jit(solution)/shard_map/psum | solution.py:145
  214.3 2.0 fusion.38
  216.4 0.7 copy.823
  217.2 2.0 copy.824
  (147 shorter events, 5.8 us)
Async XLA Ops:
  7.2 23.0 %copy-start = (f32[4,8,8,512]{3,2,1,0:T(8,128)S(1)}, f32[4,8,8,512]{3,2,1,0:T(8,128)}, u32[]{:S(2)}) copy-start(f32[4,8,8,512]{3,2,1,0:T(8,128)} %param.13) | copy-start | bytes 1572868
  7.2 10.9 %copy-start.3 = (bf16[2,8,8,128]{3,2,1,0:T(8,128)(2,1)S(1)}, bf16[2,8,8,128]{3,2,1,0:T(8,128)(2,1)}, u32[]{:S(2)}) copy-start(bf16[2,8,8,128]{3,2,1,0:T(8,128)(2,1)} %param.9) | copy-start | bytes 98308
  7.2 85.6 %all-gather.3.cloned.1.call-start = ((), (), s32[]{:S(2)}) async-start(), calls=%async_computation | async-start | bytes 3538944 | tf_op jit(solution)/shard_map/all_gather | solution.py:139
  8.0 10.6 %copy-start.4 = (f32[2,8,128]{2,1,0:T(8,128)S(1)}, f32[2,8,128]{2,1,0:T(8,128)}, u32[]{:S(2)}) copy-start(f32[2,8,128]{2,1,0:T(8,128)} %param.8) | copy-start | bytes 24580
  11.5 7.5 %copy-start.5 = (s32[2,128]{1,0:T(2,128)S(1)}, s32[2,128]{1,0:T(2,128)}, u32[]{:S(2)}) copy-start(s32[2,128]{1,0:T(2,128)} %param.10) | copy-start | bytes 3076
  19.9 75.2 %copy-start.1 = (f32[2,8,8,512]{3,2,1,0:T(8,128)S(1)}, f32[2,8,8,512]{3,2,1,0:T(8,128)}, u32[]{:S(2)}) copy-start(f32[2,8,8,512]{3,2,1,0:T(8,128)} %param.12) | copy-start | bytes 786436
  20.0 75.2 %copy-start.2 = (f32[2,8,8,512]{3,2,1,0:T(8,128)S(1)}, f32[2,8,8,512]{3,2,1,0:T(8,128)}, u32[]{:S(2)}) copy-start(f32[2,8,8,512]{3,2,1,0:T(8,128)} %param.11) | copy-start | bytes 786436
  29.9 147.3 %all-gather.5.cloned.1.call-start = ((), (), s32[]{:S(2)}) async-start(), calls=%async_computation.1 | async-start | bytes 3538944 | tf_op jit(solution)/shard_map/all_gather | solution.py:139
  118.4 95.9 %all-reduce.2.cloned.1.call-start = ((), (), s32[]{:S(2)}) async-start(), calls=%async_computation.2 | async-start | bytes 1048576 | tf_op jit(solution)/shard_map/psum | solution.py:145
Sparse Core Ops, SparseCore 0:
  30.1 62.7 all-gather.2
  118.5 58.6 all-gather.4
  182.2 32.0 all-reduce.1
